TPU v7x, 768 devices: a whole 4x8x12 slice. The times are simulated.
768 devices in a mesh: tm: 24 (over z_hi, y), head: 32 (over z_lo, x, core).
Axes of the slice: x: 4, y: 8, z: 12 (z_hi: 3, z_lo: 4; z = z_hi * 4 + z_lo), core: 2. Of those that a mesh axis runs over, the one named last changes fastest.
Arguments:
- queries: bfloat16 [49152, 4096], P('tm', 'head'), may hold values from -64 to 64
- saved_keys: bfloat16 [49152, 4096], P('tm', 'head'), may hold values from -16 to 16
- saved_values: bfloat16 [49152, 4096], P('tm', 'head'), may hold values from -6 to 6
- out_grad: bfloat16 [49152, 4096], P(('tm', 'head')), may hold values from -6 to 6
- radius: int32 [32], P('head'), may hold values from 0 to 2, as said below
- clip_ids: int32 [192], replicated, may hold values from 0 to 31, never falling along the last dimension, each value on 1 to 12 neighbouring positions
Outputs:
- grad_queries: bfloat16 [49152, 4096], P('tm', 'head')
- grad_keys: bfloat16 [49152, 4096], P('tm', 'head')
- grad_values: bfloat16 [49152, 4096], P('tm', 'head')
Inputs may be any that keep to these rules, and one draw needn't show every extreme that they name: Some head has radius exactly 2 and some head radius 0.
All inputs are finite; a program needn't handle non-finite values.
Results may differ from a plain program's by a relative error of at most 0.012.
Values may be sent and summed in bfloat16 or wider, within the bound.
No kernel may reach another device: no remote copies, remote signals or barrier semaphores. Data moves between devices by JAX's collectives and lax.ppermute only.
A program may use at most 64 MiB of HBM per device.

v0:
```python
import jax
import jax.numpy as jnp
from jax import lax
from jax.sharding import PartitionSpec as P

FRAME = 256
RADIUS = 2


def extended(array, sides, width):
    for axis, dim in sides:
        size, length = (lax.axis_size(axis), array.shape[dim])
        up = [(i, (i + 1) % size) for i in range(size - 1)]
        down = [(j, i) for i, j in up]
        last = lax.slice_in_dim(array, length - width, length, axis=dim)
        first = lax.slice_in_dim(array, 0, width, axis=dim)
        before = lax.ppermute(last, axis, up)
        after = lax.ppermute(first, axis, down)
        array = jnp.concatenate([before, array, after], axis=dim)
    return array


def passed_along(value, axis, steps):
    count = lax.axis_size(axis)
    first, last = (max(0, -steps), min(count, count - steps))
    return lax.ppermute(value, axis, [(source, source + steps) for source in range(first, last)])


def band_grads(query_rows, key_ext, value_ext, grad_rows, radius, clip_ids, first, count):
    span = 2 * RADIUS + 1
    heads = radius.shape[0]
    width = query_rows.shape[1] // heads
    scale = width ** (-0.5)
    query_blocks = query_rows.reshape(count, FRAME, heads, width)
    grad_blocks = grad_rows.reshape(count, FRAME, heads, width)
    key_frames = key_ext.reshape(count + 2 * RADIUS, FRAME, heads, width)
    value_frames = value_ext.reshape(count + 2 * RADIUS, FRAME, heads, width)
    key_window = jnp.stack([key_frames[offset : offset + count] for offset in range(span)], 1)
    value_window = jnp.stack([value_frames[offset : offset + count] for offset in range(span)], 1)
    total_frames = clip_ids.shape[0]
    table = jnp.arange(total_frames, dtype=jnp.int32)
    steps_away = jnp.arange(span, dtype=jnp.int32) - RADIUS
    query_frame = first + jnp.arange(count, dtype=jnp.int32)
    key_frame = query_frame[:, None] + steps_away[None, :]
    query_clip = jnp.sum(jnp.where(query_frame[:, None] == table, clip_ids, 0), axis=-1)
    key_clip = jnp.sum(jnp.where(key_frame[:, :, None] == table, clip_ids, 0), axis=-1)
    inside = (key_frame >= 0) & (key_frame < total_frames)
    inside = inside & (query_frame[:, None] >= 0) & (query_frame[:, None] < total_frames)
    valid = inside & (query_clip[:, None] == key_clip)
    within = jnp.abs(steps_away)[None, :] <= radius[:, None]
    allowed = valid[:, None, None, :, None] & within[None, :, None, :, None]
    scores = (
        jnp.einsum(
            "aqhd,ajkhd->ahqjk", query_blocks, key_window, preferred_element_type=jnp.float32
        )
        * scale
    )
    scores = jnp.where(allowed, scores, -1e30)
    highest = jnp.max(scores, axis=(3, 4), keepdims=True)
    expo = jnp.exp(scores - highest)
    probs = expo / jnp.sum(expo, axis=(3, 4), keepdims=True)
    probs_b = probs.astype(jnp.bfloat16)
    dprobs = jnp.einsum(
        "aqhd,ajkhd->ahqjk", grad_blocks, value_window, preferred_element_type=jnp.float32
    )
    delta = jnp.sum(probs * dprobs, axis=(3, 4), keepdims=True)
    dscores = (probs * (dprobs - delta)).astype(jnp.bfloat16)
    grad_query = (
        jnp.einsum("ahqjk,ajkhd->aqhd", dscores, key_window, preferred_element_type=jnp.float32)
        * scale
    )
    key_terms = (
        jnp.einsum("ahqjk,aqhd->ajkhd", dscores, query_blocks, preferred_element_type=jnp.float32)
        * scale
    )
    value_terms = jnp.einsum(
        "ahqjk,aqhd->ajkhd", probs_b, grad_blocks, preferred_element_type=jnp.float32
    )
    key_total = sum(
        (
            jnp.pad(key_terms[:, offset], ((offset, span - 1 - offset), (0, 0), (0, 0), (0, 0)))
            for offset in range(span)
        )
    )
    value_total = sum(
        (
            jnp.pad(value_terms[:, offset], ((offset, span - 1 - offset), (0, 0), (0, 0), (0, 0)))
            for offset in range(span)
        )
    )
    ext_rows = (count + 2 * RADIUS) * FRAME
    return (
        grad_query.reshape(count * FRAME, heads * width),
        key_total.reshape(ext_rows, heads * width),
        value_total.reshape(ext_rows, heads * width),
    )


def per_device(queries, saved_keys, saved_values, out_grad, radius, clip_ids):
    grad_heads = lax.all_to_all(out_grad, "head", split_axis=1, concat_axis=0, tiled=True)
    tm_index = lax.axis_index("tm")
    row_count = queries.shape[0]
    frame_count = row_count // FRAME
    rim = RADIUS * FRAME
    stacked = jnp.stack([saved_keys, saved_values], 0)
    widened = extended(stacked, (("tm", 1),), rim)
    grad_query, key_total, value_total = band_grads(
        queries,
        widened[0],
        widened[1],
        grad_heads,
        radius,
        clip_ids,
        tm_index * frame_count,
        frame_count,
    )
    terms = jnp.stack([key_total, value_total], 0)
    from_next = passed_along(terms[:, :rim].astype(jnp.bfloat16), "tm", -1).astype(jnp.float32)
    from_previous = passed_along(terms[:, rim + row_count :].astype(jnp.bfloat16), "tm", 1).astype(
        jnp.float32
    )
    middle = terms[:, rim : rim + row_count]
    owned = jnp.concatenate(
        [
            middle[:, :rim] + from_previous,
            middle[:, rim : row_count - rim],
            middle[:, row_count - rim :] + from_next,
        ],
        1,
    )
    grad_key = owned[0]
    grad_value = owned[1]
    return (
        grad_query.astype(jnp.bfloat16),
        grad_key.astype(jnp.bfloat16),
        grad_value.astype(jnp.bfloat16),
    )


def solution(mesh):
    placed = (
        P("tm", "head"),
        P("tm", "head"),
        P("tm", "head"),
        P(("tm", "head"), None),
        P("head"),
        P(),
    )
    return jax.shard_map(
        per_device,
        mesh=mesh,
        in_specs=placed,
        out_specs=(P("tm", "head"), P("tm", "head"), P("tm", "head")),
        check_vma=False,
    )
```

profile of v0, /device:TPU:319, one launch (start us, length us, event | category | flops | bytes accessed | tf_op | source)
XLA Modules:
  0.0 117.2 jit_solution(16227186470695703796)
XLA Ops:
  0.7 1.2 %pad_maximum_fusion.2 = (bf16[2,512,128]{2,1,0:T(8,128)(2,1)S(1)}, bf16[2,512,128]{2,1,0:T(8,128)(2,1)S(1)}) fusion(bf16[1,2048,128]{2,1,0:T(8,128)(2,1)} %bitcast.161, bf16[1,2048,128]{2,1,0:T(8,128)(2,1)} %bitcast.158), kind=kLoop, calls=%fused_computation.56 | loop fusion | flops 1048576 | bytes 1572864 | tf_op jit(solution)/shard_map/stack | solution.py:105
  1.8 3.0 %collective-permute-start.1 = (bf16[2,512,128]{2,1,0:T(8,128)(2,1)S(1)}, bf16[2,512,128]{2,1,0:T(8,128)(2,1)S(1)}, u32[]{:S(2)}, u32[]{:S(2)}) collective-permute-start(bf16[2,512,128]{2,1,0:T(8,128)(2,1)S(1)} %get-tuple-element.29), channel_id=1, source_target_pairs={{32,0},{64,32},{96,64},{128,96},{160,128},{192,160},{224,192},{256... | collective-permute-start | bytes 786440 | tf_op jit(solution)/shard_map/ppermute | solution.py:18
  4.8 8.3 %collective-permute-start = (bf16[2,512,128]{2,1,0:T(8,128)(2,1)S(1)}, bf16[2,512,128]{2,1,0:T(8,128)(2,1)}, u32[]{:S(2)}, u32[]{:S(2)}) collective-permute-start(bf16[2,512,128]{2,1,0:T(8,128)(2,1)S(1)} %get-tuple-element.30), channel_id=1, source_target_pairs={{0,32},{32,64},{64,96},{96,128},{128,160},{160,192},{192,224},{224... | collective-permute-start | bytes 786440 | tf_op jit(solution)/shard_map/ppermute | solution.py:17
  13.2 2.0 %copy_bitcast_fusion = bf16[64,32,128]{2,0,1:T(8,128)(2,1)} fusion(bf16[64,4096]{1,0:T(8,128)(2,1)} %param.9), kind=kLoop, calls=%fused_computation.53 | loop fusion | bytes 1048576 | tf_op jit(solution)/shard_map/all_to_all | solution.py:100
  15.1 11.0 %all-to-all-start = ((bf16[64,32,128]{2,0,1:T(8,128)(2,1)}), bf16[64,32,128]{2,0,1:T(8,128)(2,1)}, u32[]{:S(2)}, u32[]{:S(2)}) async-start(bf16[64,32,128]{2,0,1:T(8,128)(2,1)} %copy_bitcast_fusion), calls=%async_computation | async-start | bytes 1048576 | tf_op jit(solution)/shard_map/all_to_all | solution.py:100
  27.5 6.0 %collective-permute-done.1 = bf16[2,512,128]{2,1,0:T(8,128)(2,1)S(1)} collective-permute-done((bf16[2,512,128]{2,1,0:T(8,128)(2,1)S(1)}, bf16[2,512,128]{2,1,0:T(8,128)(2,1)S(1)}, u32[]{:S(2)}, u32[]{:S(2)}) %collective-permute-start.1) | collective-permute-done | bytes 262176 | tf_op jit(solution)/shard_map/ppermute | solution.py:18
  34.5 1.9 %pad_maximum_fusion.1 = (bf16[2,2560,128]{2,1,0:T(8,128)(2,1)S(1)}, bf16[2,2560,128]{2,1,0:T(8,128)(2,1)S(1)}) fusion(bf16[2,512,128]{2,1,0:T(8,128)(2,1)S(1)} %collective-permute-done.1, bf16[1,2048,128]{2,1,0:T(8,128)(2,1)} %bitcast.162, bf16[1,2048,128]{2,1,0:T(8,128)(2,1)} %bitcast.159, bf16[2,512,128]{2,1,0:T(8,128)(2,1)} %collective-permute-done), kind=kLoop, calls=%fused_computation.35 | loop fusion | flops 7864320 | bytes 4194304 | tf_op jit(solution)/shard_map/concatenate | solution.py:19
  38.5 1.5 %copy-done.10 = bf16[8,5,256,1,128]{4,2,1,0,3:T(8,128)(2,1)} copy-done((bf16[8,5,256,1,128]{4,2,1,0,3:T(8,128)(2,1)}, bf16[8,5,256,1,128]{4,2,1,0,3:T(8,128)(2,1)S(1)}, u32[]{:S(2)}) %copy-start.10) | copy-done | bytes 2621464
  39.9 1.5 %bitcast_reduce_fusion = (f32[8,256]{1,0:T(8,128)S(1)}, f32[8,5,256,256]{3,2,1,0:T(8,128)S(1)}) fusion(pred[8,5]{1,0:T(8,128)(4,1)S(1)} %copy.32, bf16[8,256,128,1]{2,1,3,0:T(8,128)(2,1)S(1)} %bitcast.150, bf16[8,5,256,1,128]{4,2,1,0,3:T(8,128)(2,1)S(1)} %constant_dynamic-update-slice_fusion), kind=kOutput, calls=%fused_computation.6 | convolution fusion | flops 678950912 | bytes 13639720 | tf_op jit(solution)/shard_map/aqhd,ajkhd->ahqjk/dot_general | solution.py:53
  41.5 4.0 %copy-done.1 = f32[8,5,256,256]{3,2,1,0:T(8,128)} copy-done((f32[8,5,256,256]{3,2,1,0:T(8,128)}, f32[8,5,256,256]{3,2,1,0:T(8,128)S(1)}, u32[]{:S(2)}) %copy-start.1) | copy-done | bytes 10485784
  45.5 2.4 %fusion.5 = f32[8,256]{1,0:T(8,128)S(1)} fusion(f32[8,5,256,256]{3,2,1,0:T(8,128)S(1)} %get-tuple-element.32, f32[8,256]{1,0:T(8,128)S(1)} %get-tuple-element.31, pred[8,5]{1,0:T(8,128)(4,1)S(1)} %copy.32), kind=kLoop, calls=%fused_computation.10 | loop fusion | flops 10483712 | bytes 10502184 | tf_op jit(solution)/shard_map/reduce_sum | solution.py:61
  47.9 9.0 %fusion.15 = f32[8,5,256,1,128]{4,2,1,0,3:T(8,128)} fusion(bf16[8,256,128,1]{2,1,3,0:T(8,128)(2,1)} %bitcast.22, f32[8,5,256,256]{3,2,1,0:T(8,128)} %copy-done.1, f32[8,256]{1,0:T(8,128)S(1)} %fusion.5, f32[8,256]{1,0:T(8,128)S(1)} %get-tuple-element.31, pred[8,5]{1,0:T(8,128)(4,1)S(1)} %copy.32), kind=kOutput, calls=%fused_computation.28 | convolution fusion | flops 684195840 | bytes 16269352 | tf_op jit(solution)/shard_map/ahqjk,aqhd->ajkhd/dot_general | solution.py:76
  56.9 4.5 %fusion = (f32[8,256]{1,0:T(8,128)S(1)}, f32[8,5,256,256]{3,2,1,0:T(8,128)S(1)}) fusion(f32[8,256]{1,0:T(8,128)S(1)} %fusion.5, f32[8,256]{1,0:T(8,128)S(1)} %get-tuple-element.31, f32[8,5,256,256]{3,2,1,0:T(8,128)S(1)} %copy-done.2, pred[8,5]{1,0:T(8,128)(4,1)S(1)} %copy.32, bf16[8,256,128,1]{2,1,3,0:T(8,128)(2,1)} %bitcast.22, ...), kind=kOutput, calls=%fused_computation.2 | convolution fusion | flops 686815232 | bytes 24141864 | tf_op jit(solution)/shard_map/aqhd,ajkhd->ahqjk/dot_general | solution.py:63
  61.4 4.1 %fusion.2 = bf16[8,256,5,256]{1,3,2,0:T(8,128)(2,1)S(1)} fusion(f32[8,5,256,256]{3,2,1,0:T(8,128)S(1)} %get-tuple-element.34, f32[8,256]{1,0:T(8,128)S(1)} %get-tuple-element.33, f32[8,256]{1,0:T(8,128)S(1)} %fusion.5, f32[8,256]{1,0:T(8,128)S(1)} %get-tuple-element.31, f32[8,5,256,256]{3,2,1,0:T(8,128)S(1)} %copy-done.2, pred[8,5]{1,0:T(8,128)(4,1)S(1)} %copy.32), kind=kLoop, calls=%fused_computation.4 | loop fusion | flops 18350080 | bytes 26239016 | tf_op jit(solution)/shard_map/convert_element_type | solution.py:67
  65.5 1.5 %multiply_bitcast_fusion = f32[8,5,256,1,128]{4,2,1,0,3:T(8,128)S(1)} fusion(bf16[8,256,5,256]{1,3,2,0:T(8,128)(2,1)S(1)} %fusion.2, bf16[8,256,128,1]{2,1,3,0:T(8,128)(2,1)S(1)} %bitcast.151), kind=kOutput, calls=%fused_computation.13 | convolution fusion | flops 672399360 | bytes 11010048 | tf_op jit(solution)/shard_map/ahqjk,aqhd->ajkhd/dot_general | solution.py:73
  67.6 1.9 %copy-done.7 = f32[8,5,256,1,128]{4,2,1,0,3:T(8,128)S(1)} copy-done((f32[8,5,256,1,128]{4,2,1,0,3:T(8,128)S(1)}, f32[8,5,256,1,128]{4,2,1,0,3:T(8,128)}, u32[]{:S(2)}) %copy-start.7) | copy-done | bytes 5242904
  72.6 10.2 %collective-permute-start.2 = (bf16[2,512,128]{2,1,0:T(8,128)(2,1)}, bf16[2,512,128]{2,1,0:T(8,128)(2,1)S(1)}, u32[]{:S(2)}, u32[]{:S(2)}) collective-permute-start(bf16[2,512,128]{2,1,0:T(8,128)(2,1)} %get-tuple-element.15), channel_id=1, source_target_pairs={{0,32},{32,64},{64,96},{96,128},{128,160},{160,192},{192,224},{224... | collective-permute-start | bytes 786440 | tf_op jit(solution)/shard_map/ppermute | solution.py:26
  82.9 1.9 %collective-permute-start.3 = (bf16[2,512,128]{2,1,0:T(8,128)(2,1)}, bf16[2,512,128]{2,1,0:T(8,128)(2,1)}, u32[]{:S(2)}, u32[]{:S(2)}) collective-permute-start(bf16[2,512,128]{2,1,0:T(8,128)(2,1)} %get-tuple-element.16), channel_id=1, source_target_pairs={{32,0},{64,32},{96,64},{128,96},{160,128},{192,160},{224,192},{256... | collective-permute-start | bytes 786440 | tf_op jit(solution)/shard_map/ppermute | solution.py:26
  84.8 1.9 %fusion.27 = bf16[8,256,1,128]{1,3,0,2:T(8,128)(2,1)} fusion(bf16[8,256,5,256]{1,3,2,0:T(8,128)(2,1)S(1)} %fusion.2, bf16[8,5,256,1,128]{4,2,1,0,3:T(8,128)(2,1)S(1)} %constant_dynamic-update-slice_fusion), kind=kOutput, calls=%fused_computation.37 | convolution fusion | flops 671612928 | bytes 8388608 | tf_op jit(solution)/shard_map/ahqjk,ajkhd->aqhd/dot_general | solution.py:69
  86.7 2.2 %copy.36 = bf16[8,256,1,128]{3,1,0,2:T(8,128)(2,1)} copy(bf16[8,256,1,128]{1,3,0,2:T(8,128)(2,1)} %fusion.27) | data formatting | bytes 1048576 | tf_op jit(solution)/shard_map/convert_element_type | solution.py:134
  88.9 1.4 %fusion.30 = bf16[2,1024,128]{2,1,0:T(8,128)(2,1)S(1)} fusion(f32[1,3072,128]{2,1,0:T(8,128)} %bitcast.153, f32[1,3072,128]{2,1,0:T(8,128)} %bitcast.156), kind=kLoop, calls=%fused_computation.38 | loop fusion | flops 262144 | bytes 3670016 | tf_op jit(solution)/shard_map/stack | solution.py:117
  90.3 13.0 %collective-permute-done.2 = bf16[2,512,128]{2,1,0:T(8,128)(2,1)S(1)} collective-permute-done((bf16[2,512,128]{2,1,0:T(8,128)(2,1)}, bf16[2,512,128]{2,1,0:T(8,128)(2,1)S(1)}, u32[]{:S(2)}, u32[]{:S(2)}) %collective-permute-start.2) | collective-permute-done | bytes 262176 | tf_op jit(solution)/shard_map/ppermute | solution.py:26
  103.3 11.8 %collective-permute-done.3 = bf16[2,512,128]{2,1,0:T(8,128)(2,1)} collective-permute-done((bf16[2,512,128]{2,1,0:T(8,128)(2,1)}, bf16[2,512,128]{2,1,0:T(8,128)(2,1)}, u32[]{:S(2)}, u32[]{:S(2)}) %collective-permute-start.3) | collective-permute-done | bytes 262176 | tf_op jit(solution)/shard_map/ppermute | solution.py:26
  115.1 1.1 fusion.32
  (51 shorter events, 8.5 us)
Async XLA Ops:
  0.6 39.3 %copy-start = (bf16[2048,128]{1,0:T(8,128)(2,1)S(1)}, bf16[2048,128]{1,0:T(8,128)(2,1)}, u32[]{:S(2)}) copy-start(bf16[2048,128]{1,0:T(8,128)(2,1)} %param.6) | copy-start | bytes 1572868
  0.6 25.6 %copy-start.11 = (s32[192]{0:T(256)S(1)}, s32[192]{0:T(256)}, u32[]{:S(2)}) copy-start(s32[192]{0:T(256)} %param.11) | copy-start | bytes 2308
  1.8 31.6 %collective-permute-start.1 = (bf16[2,512,128]{2,1,0:T(8,128)(2,1)S(1)}, bf16[2,512,128]{2,1,0:T(8,128)(2,1)S(1)}, u32[]{:S(2)}, u32[]{:S(2)}) collective-permute-start(bf16[2,512,128]{2,1,0:T(8,128)(2,1)S(1)} %get-tuple-element.29), channel_id=1, source_target_pairs={{32,0},{64,32},{96,64},{128,96},{160,128},{192,160},{224,192},{256... | collective-permute-start | bytes 786440 | tf_op jit(solution)/shard_map/ppermute | solution.py:18
  4.8 29.7 %collective-permute-start = (bf16[2,512,128]{2,1,0:T(8,128)(2,1)S(1)}, bf16[2,512,128]{2,1,0:T(8,128)(2,1)}, u32[]{:S(2)}, u32[]{:S(2)}) collective-permute-start(bf16[2,512,128]{2,1,0:T(8,128)(2,1)S(1)} %get-tuple-element.30), channel_id=1, source_target_pairs={{0,32},{32,64},{64,96},{96,128},{128,160},{160,192},{192,224},{224... | collective-permute-start | bytes 786440 | tf_op jit(solution)/shard_map/ppermute | solution.py:17
  15.1 32.7 %all-to-all-start = ((bf16[64,32,128]{2,0,1:T(8,128)(2,1)}), bf16[64,32,128]{2,0,1:T(8,128)(2,1)}, u32[]{:S(2)}, u32[]{:S(2)}) async-start(bf16[64,32,128]{2,0,1:T(8,128)(2,1)} %copy_bitcast_fusion), calls=%async_computation | async-start | bytes 1048576 | tf_op jit(solution)/shard_map/all_to_all | solution.py:100
  36.9 1.0 copy-start.8
  37.0 1.3 %copy-start.9 = (bf16[2048,128]{1,0:T(8,128)(2,1)S(1)}, bf16[2048,128]{1,0:T(8,128)(2,1)}, u32[]{:S(2)}) copy-start(bf16[2048,128]{1,0:T(8,128)(2,1)} %param.8) | copy-start | bytes 1572868
  38.4 1.5 %copy-start.10 = (bf16[8,5,256,1,128]{4,2,1,0,3:T(8,128)(2,1)}, bf16[8,5,256,1,128]{4,2,1,0,3:T(8,128)(2,1)S(1)}, u32[]{:S(2)}) copy-start(bf16[8,5,256,1,128]{4,2,1,0,3:T(8,128)(2,1)S(1)} %constant_dynamic-update-slice_fusion.5) | copy-start | bytes 7864324
  41.5 4.0 %copy-start.1 = (f32[8,5,256,256]{3,2,1,0:T(8,128)}, f32[8,5,256,256]{3,2,1,0:T(8,128)S(1)}, u32[]{:S(2)}) copy-start(f32[8,5,256,256]{3,2,1,0:T(8,128)S(1)} %get-tuple-element.32) | copy-start | bytes 31457284
  47.9 9.0 %copy-start.2 = (f32[8,5,256,256]{3,2,1,0:T(8,128)S(1)}, f32[8,5,256,256]{3,2,1,0:T(8,128)}, u32[]{:S(2)}) copy-start(f32[8,5,256,256]{3,2,1,0:T(8,128)} %copy-done.1) | copy-start | bytes 31457284
  67.0 2.5 %copy-start.7 = (f32[8,5,256,1,128]{4,2,1,0,3:T(8,128)S(1)}, f32[8,5,256,1,128]{4,2,1,0,3:T(8,128)}, u32[]{:S(2)}) copy-start(f32[8,5,256,1,128]{4,2,1,0,3:T(8,128)} %fusion.15) | copy-start | bytes 15728644
  70.4 1.2 copy-start.3
  70.7 2.0 %copy-start.5 = (f32[12,256,1,128]{3,1,0,2:T(8,128)}, f32[12,256,1,128]{3,1,0,2:T(8,128)S(1)}, u32[]{:S(2)}) copy-start(f32[12,256,1,128]{3,1,0,2:T(8,128)S(1)} %pad_add_fusion) | copy-start | bytes 4718596
  72.6 30.6 %collective-permute-start.2 = (bf16[2,512,128]{2,1,0:T(8,128)(2,1)}, bf16[2,512,128]{2,1,0:T(8,128)(2,1)S(1)}, u32[]{:S(2)}, u32[]{:S(2)}) collective-permute-start(bf16[2,512,128]{2,1,0:T(8,128)(2,1)} %get-tuple-element.15), channel_id=1, source_target_pairs={{0,32},{32,64},{64,96},{96,128},{128,160},{160,192},{192,224},{224... | collective-permute-start | bytes 786440 | tf_op jit(solution)/shard_map/ppermute | solution.py:26
  82.9 32.2 %collective-permute-start.3 = (bf16[2,512,128]{2,1,0:T(8,128)(2,1)}, bf16[2,512,128]{2,1,0:T(8,128)(2,1)}, u32[]{:S(2)}, u32[]{:S(2)}) collective-permute-start(bf16[2,512,128]{2,1,0:T(8,128)(2,1)} %get-tuple-element.16), channel_id=1, source_target_pairs={{32,0},{64,32},{96,64},{128,96},{160,128},{192,160},{224,192},{256... | collective-permute-start | bytes 786440 | tf_op jit(solution)/shard_map/ppermute | solution.py:26
  86.7 28.3 %copy-start.4 = (f32[12,256,1,128]{3,1,0,2:T(8,128)S(1)}, f32[12,256,1,128]{3,1,0,2:T(8,128)}, u32[]{:S(2)}) copy-start(f32[12,256,1,128]{3,1,0,2:T(8,128)} %copy-done.3) | copy-start | bytes 4718596
  88.9 26.2 %copy-start.6 = (f32[12,256,1,128]{3,1,0,2:T(8,128)S(1)}, f32[12,256,1,128]{3,1,0,2:T(8,128)}, u32[]{:S(2)}) copy-start(f32[12,256,1,128]{3,1,0,2:T(8,128)} %copy-done.5) | copy-start | bytes 4718596
where the time goes:
time: 118 us; the launch traced here: 117 us
  starting transfers between devices  34.4 us (29%)
  waiting for transfers between devices  31.8 us (27%)
  matrix products  18.5 us (16%)
  local copies, waits for them, and re-layouts  17.5 us (15%)
  other arithmetic  13.4 us (11%)
  between operations  1.65 us (1%)
    ppermute x2, waiting for transfers between devices, passed_along(): lax.ppermute(value, axis, [(source, source + steps) for source in range(f...  24.8 us
    ppermute x2, starting transfers between devices, passed_along(): lax.ppermute(value, axis, [(source, source + steps) for source in range(f...  12.1 us
    all_to_all x1, starting transfers between devices, per_device(): lax.all_to_all(out_grad, 'head', split_axis=1, concat_axis=0, tiled=True)  11 us
    unnamed x32, local copies, waits for them, and re-layouts  9.61 us
    dot_general x1, matrix products, band_grads(): jnp.einsum('ahqjk,aqhd->ajkhd', probs_b, grad_blocks, preferred_element_t...  9 us
    ppermute x1, starting transfers between devices, extended(): before = lax.ppermute(last, axis, up)  8.32 us
    ppermute x1, waiting for transfers between devices, extended(): after = lax.ppermute(first, axis, down)  5.98 us
    dot_general x1, matrix products, band_grads(): jnp.einsum('aqhd,ajkhd->ahqjk', grad_blocks, value_window, preferred_elem...  4.47 us
  transfers between devices with their start and end apart: 5, of which 4 were waited for; matrix products, arithmetic and copies ran while one was open for 13% of the time, Pallas kernels for 0%

commit v1 on v0

v1 whole, which is shorter than its diff:
```python
import functools

import jax
import jax.numpy as jnp
from jax import lax
from jax.experimental import pallas as pl
from jax.experimental.pallas import tpu as pltpu
from jax.sharding import PartitionSpec as P


FRAME = 256
RADIUS = 2
SPAN = 2 * RADIUS + 1
NEG = -1e30
LOG2E = 1.4426950408889634
STAT_ROWS = 48

NT = (((1,), (1,)), ((), ()))
NN = (((1,), (0,)), ((), ()))


def dot(a, b, dims):
    return lax.dot_general(a, b, dims, preferred_element_type=jnp.float32)


def frame_rows(index):
    return pl.ds(pl.multiple_of(index * FRAME, FRAME), FRAME)


def make_allowed(where_ref, radius_ref, clip_ref, count):
    first = where_ref[0] * count
    total = clip_ref.shape[0]
    radius = radius_ref[0]

    def allowed(query, key):
        fq = first + query
        fk = first + key
        inside = (fq >= 0) & (fq < total) & (fk >= 0) & (fk < total)
        cq = clip_ref[jnp.clip(fq, 0, total - 1)]
        ck = clip_ref[jnp.clip(fk, 0, total - 1)]
        return inside & (jnp.abs(fq - fk) <= radius) & (cq == ck)

    return allowed


def stats_kernel(count, where_ref, radius_ref, clip_ref, q_ref, k_ref, v_ref, g_ref, odd_ref, even_ref, e_scr, row_scr):
    width = q_ref.shape[1]
    c = width**-0.5 * LOG2E
    allowed = make_allowed(where_ref, radius_ref, clip_ref, count)
    parity = lax.rem(where_ref[0], 2)
    row_scr[...] = jnp.zeros_like(row_scr)
    for slot, out in ((0, odd_ref), (1, even_ref)):
        side = parity if slot == 0 else 1 - parity
        base_q = side * (count - RADIUS)
        base_k = side * (count - 2 * RADIUS)
        for i in range(RADIUS):
            qf = base_q + i
            q = q_ref[frame_rows(qf), :]
            g = g_ref[frame_rows(qf), :]
            out[i * FRAME : (i + 1) * FRAME, :] = g
            top = None
            for j in range(2 * RADIUS):
                s = dot(k_ref[frame_rows(base_k + j), :], q, NT)
                s = jnp.where(allowed(qf, base_k + j), s, NEG)
                e_scr[j] = s
                peak = jnp.max(s, axis=0, keepdims=True)
                top = peak if top is None else jnp.maximum(top, peak)
            total = jnp.zeros_like(top)
            delta = jnp.zeros_like(top)
            for j in range(2 * RADIUS):
                e = jnp.exp2((e_scr[j] - top) * c)
                dp = dot(v_ref[frame_rows(base_k + j), :], g, NT)
                total = total + jnp.sum(e, axis=0, keepdims=True)
                delta = delta + jnp.sum(e * dp, axis=0, keepdims=True)
            row = i * 18
            for stat in (top, total, delta):
                rest = stat
                for _ in range(3):
                    part = rest.astype(jnp.bfloat16).astype(jnp.float32)
                    rest = rest - part
                    row_scr[row : row + 1, :] = part[:, :128]
                    row_scr[row + 1 : row + 2, :] = part[:, 128:]
                    row += 2
        out[RADIUS * FRAME :, :] = row_scr[...].astype(jnp.bfloat16)


def main_kernel(
    count,
    where_ref,
    radius_ref,
    clip_ref,
    q_ref,
    k_ref,
    v_ref,
    g_ref,
    odd_ref,
    even_ref,
    relay_ref,
    godd_ref,
    geven_ref,
    dq_ref,
    dk_ref,
    dv_ref,
    kx,
    vx,
    qx,
    gx,
    kt,
    dk_acc,
    dv_acc,
    e_scr,
    dp_scr,
    stat_scr,
):
    width = q_ref.shape[1]
    scale = width**-0.5
    c = scale * LOG2E
    rim = RADIUS * FRAME
    own = count * FRAME
    allowed = make_allowed(where_ref, radius_ref, clip_ref, count)
    parity = lax.rem(where_ref[0], 2)
    kx[pl.ds(rim, own), :] = k_ref[...]
    vx[pl.ds(rim, own), :] = v_ref[...]
    far = where_ref[1]
    for slot, kvq, gs in ((0, odd_ref, godd_ref), (1, even_ref, geven_ref)):
        after = parity if slot == 0 else 1 - parity
        dst = pl.ds(pl.multiple_of(after * (rim + own), rim), rim)
        half = pl.ds(pl.multiple_of(after * rim, rim), rim)
        kx[dst, :] = kvq[0:rim, :]
        vx[dst, :] = kvq[rim : 2 * rim, :]
        qx[half, :] = kvq[2 * rim : 3 * rim, :]
        if slot == 0:

            @pl.when(far == 1)
            def _():
                vx[dst, :] = relay_ref[0:rim, :]
                qx[half, :] = relay_ref[rim : 2 * rim, :]

        gx[half, :] = gs[0:rim, :]
        stat_scr[pl.ds(pl.multiple_of(after * STAT_ROWS, 8), STAT_ROWS), :] = gs[rim:, :].astype(jnp.float32)
    for f in range(count + 2 * RADIUS):
        kt[:, f * FRAME : (f + 1) * FRAME] = kx[f * FRAME : (f + 1) * FRAME, :].T
    dk_acc[...] = jnp.zeros_like(dk_acc)
    dv_acc[...] = jnp.zeros_like(dv_acc)

    def one_query_frame(a, carry):
        q = q_ref[frame_rows(a), :]
        g = g_ref[frame_rows(a), :]
        top = None
        for j in range(SPAN):
            s = dot(kx[frame_rows(a + j), :], q, NT)
            s = jnp.where(allowed(a, a + j - RADIUS), s, NEG)
            e_scr[j] = s
            peak = jnp.max(s, axis=0, keepdims=True)
            top = peak if top is None else jnp.maximum(top, peak)
        total = jnp.zeros_like(top)
        delta = jnp.zeros_like(top)
        for j in range(SPAN):
            e = jnp.exp2((e_scr[j] - top) * c)
            dp = dot(vx[frame_rows(a + j), :], g, NT)
            total = total + jnp.sum(e, axis=0, keepdims=True)
            delta = delta + jnp.sum(e * dp, axis=0, keepdims=True)
            e_scr[j] = e
            dp_scr[j] = dp
        inverse = 1.0 / total
        delta = delta * inverse
        dqt = None
        for j in range(SPAN):
            p = e_scr[j] * inverse
            ds = (p * (dp_scr[j] - delta)).astype(jnp.bfloat16)
            rows = frame_rows(a + j)
            dv_acc[rows, :] += dot(p.astype(jnp.bfloat16), g, NN)
            dk_acc[rows, :] += dot(ds, q, NN)
            part = dot(kt[:, rows], ds, NN)
            dqt = part if dqt is None else dqt + part
        dq_ref[frame_rows(a), :] = (dqt * scale).T.astype(jnp.bfloat16)
        return carry

    lax.fori_loop(0, count, one_query_frame, 0)

    for h in range(2 * RADIUS):
        side, i = divmod(h, RADIUS)
        if side == 0:
            qf = i - RADIUS
            keys = list(range(0, i + 1))
        else:
            qf = count + i
            keys = list(range(count - RADIUS + i, count))
        q = qx[h * FRAME : (h + 1) * FRAME, :]
        g = gx[h * FRAME : (h + 1) * FRAME, :]
        stats = []
        row = side * STAT_ROWS + i * 18
        for _ in range(3):
            halves = []
            for lane in range(2):
                halves.append(
                    stat_scr[row + lane : row + lane + 1, :]
                    + stat_scr[row + 2 + lane : row + 3 + lane, :]
                    + stat_scr[row + 4 + lane : row + 5 + lane, :]
                )
            stats.append(jnp.concatenate(halves, axis=1))
            row += 6
        far_top, far_total, far_delta = stats
        top = far_top
        for n, f in enumerate(keys):
            s = dot(k_ref[f * FRAME : (f + 1) * FRAME, :], q, NT)
            s = jnp.where(allowed(qf, f), s, NEG)
            e_scr[n] = s
            top = jnp.maximum(top, jnp.max(s, axis=0, keepdims=True))
        fade = jnp.exp2((far_top - top) * c)
        total = far_total * fade
        delta = far_delta * fade
        for n, f in enumerate(keys):
            e = jnp.exp2((e_scr[n] - top) * c)
            dp = dot(v_ref[f * FRAME : (f + 1) * FRAME, :], g, NT)
            total = total + jnp.sum(e, axis=0, keepdims=True)
            delta = delta + jnp.sum(e * dp, axis=0, keepdims=True)
            e_scr[n] = e
            dp_scr[n] = dp
        inverse = jnp.where(total > 0.0, 1.0 / total, 0.0)
        delta = delta * inverse
        for n, f in enumerate(keys):
            p = e_scr[n] * inverse
            ds = (p * (dp_scr[n] - delta)).astype(jnp.bfloat16)
            rows = slice((f + RADIUS) * FRAME, (f + RADIUS + 1) * FRAME)
            dv_acc[rows, :] += dot(p.astype(jnp.bfloat16), g, NN)
            dk_acc[rows, :] += dot(ds, q, NN)
    dk_ref[...] = (dk_acc[pl.ds(rim, own), :] * scale).astype(jnp.bfloat16)
    dv_ref[...] = dv_acc[pl.ds(rim, own), :].astype(jnp.bfloat16)


VM = pl.BlockSpec(memory_space=pltpu.VMEM)
SM = pl.BlockSpec(memory_space=pltpu.SMEM)


def stats_call(where, radius, clip_ids, q, k, v, g):
    rows, width = q.shape
    count = rows // FRAME
    out = jax.ShapeDtypeStruct((RADIUS * FRAME + STAT_ROWS, width), jnp.bfloat16)
    return pl.pallas_call(
        functools.partial(stats_kernel, count),
        out_shape=(out, out),
        in_specs=[SM] * 3 + [VM] * 4,
        out_specs=(VM, VM),
        scratch_shapes=[
            pltpu.VMEM((2 * RADIUS, FRAME, FRAME), jnp.float32),
            pltpu.VMEM((STAT_ROWS, width), jnp.float32),
        ],
        cost_estimate=pl.CostEstimate(flops=16 * 4 * FRAME * FRAME * width, bytes_accessed=5 * rows * width, transcendentals=0),
        name="rim_stats",
    )(where, radius, clip_ids, q, k, v, g)


def main_call(where, radius, clip_ids, q, k, v, g, odd, even, relay, godd, geven):
    rows, width = q.shape
    count = rows // FRAME
    ext = rows + 2 * RADIUS * FRAME
    out = jax.ShapeDtypeStruct((rows, width), jnp.bfloat16)
    return pl.pallas_call(
        functools.partial(main_kernel, count),
        out_shape=(out, out, out),
        in_specs=[SM] * 3 + [VM] * 9,
        out_specs=(VM, VM, VM),
        scratch_shapes=[
            pltpu.VMEM((ext, width), jnp.bfloat16),
            pltpu.VMEM((ext, width), jnp.bfloat16),
            pltpu.VMEM((2 * RADIUS * FRAME, width), jnp.bfloat16),
            pltpu.VMEM((2 * RADIUS * FRAME, width), jnp.bfloat16),
            pltpu.VMEM((width, ext), jnp.bfloat16),
            pltpu.VMEM((ext, width), jnp.float32),
            pltpu.VMEM((ext, width), jnp.float32),
            pltpu.VMEM((SPAN, FRAME, FRAME), jnp.float32),
            pltpu.VMEM((SPAN, FRAME, FRAME), jnp.float32),
            pltpu.VMEM((2 * STAT_ROWS, width), jnp.float32),
        ],
        cost_estimate=pl.CostEstimate(flops=46 * 10 * FRAME * FRAME * width, bytes_accessed=14 * rows * width, transcendentals=0),
        name="band_grads",
    )(where, radius, clip_ids, q, k, v, g, odd, even, relay, godd, geven)


def both_ways(pairs):
    return pairs + [(b, a) for a, b in pairs]


def exchange_pairs(size, plane):
    odd = both_ways([(i, i + 1) for i in range(1, size - 1, 2)])
    even = both_ways([(i, i + 1) for i in range(0, size - 1, 2)])
    far = [(i, i + 1) for i in range(plane - 1, size - 1, plane)]
    near_odd = [p for p in odd if p not in both_ways(far)]
    first, second, third = [], [], []
    for a, b in far:
        low, high = a - plane + 1, b + plane - 1
        first += [(a, low), (b, high)]
        second += [(low, b), (high, a)]
        third += [(a - 1, b), (b + 1, a)]
    return odd, near_odd, even, far, first, second, third


def per_device(queries, saved_keys, saved_values, out_grad, radius, clip_ids):
    size = lax.axis_size("tm")
    tm = lax.axis_index("tm")
    rows = queries.shape[0]
    rim = RADIUS * FRAME
    parity = tm % 2
    odd_pairs, near_pairs, even_pairs, far_pairs, hop_a1, hop_a2, hop_b2 = exchange_pairs(size, 8)
    is_far = sum((tm == i).astype(jnp.int32) for pair in far_pairs for i in pair)
    where = jnp.stack([tm.astype(jnp.int32), is_far])

    def rim_of(x, slot):
        last = parity if slot == 0 else 1 - parity
        return lax.dynamic_slice_in_dim(x, last * (rows - rim), rim, 0)

    grads = lax.all_to_all(out_grad, "head", split_axis=1, concat_axis=0, tiled=True)
    k_odd, v_odd, q_odd = (rim_of(x, 0) for x in (saved_keys, saved_values, queries))
    relay_v = lax.ppermute(v_odd, "tm", hop_a1)
    even = lax.ppermute(jnp.concatenate([rim_of(x, 1) for x in (saved_keys, saved_values, queries)] + [q_odd], 0), "tm", even_pairs)
    odd_k = lax.ppermute(k_odd, "tm", odd_pairs)
    odd_vq = lax.ppermute(jnp.concatenate([v_odd, q_odd], 0), "tm", near_pairs)
    relay_v = lax.ppermute(relay_v, "tm", hop_a2)
    relay_q = lax.ppermute(even[3 * rim :], "tm", hop_b2)
    relay = jnp.concatenate([relay_v, relay_q], 0)
    odd = jnp.concatenate([odd_k, odd_vq], 0)
    godd, geven = stats_call(where, radius, clip_ids, queries, saved_keys, saved_values, grads)
    godd = lax.ppermute(godd, "tm", odd_pairs)
    geven = lax.ppermute(geven, "tm", even_pairs)
    return main_call(where, radius, clip_ids, queries, saved_keys, saved_values, grads, odd, even, relay, godd, geven)


def solution(mesh):
    placed = (P("tm", "head"),) * 3 + (P(("tm", "head"), None), P("head"), P())
    return jax.shard_map(
        per_device,
        mesh=mesh,
        in_specs=placed,
        out_specs=(P("tm", "head"),) * 3,
        check_vma=False,
    )
```

time: 118 us -> 83 us (0.70)
  the two profiles are of different devices: /device:TPU:319 before, /device:TPU:58 now
where the time goes in v1:
time: 83 us; the launch traced here: 82.5 us
  starting transfers between devices  44.2 us (53%)
  Pallas kernels  20.6 us (25%)
  waiting for transfers between devices  8.83 us (11%)
  local copies, waits for them, and re-layouts  5.26 us (6%)
  other arithmetic  2.15 us (3%)
  between operations  1.52 us (2%)
    pallas_call x1, Pallas kernels, main_call(): pl.pallas_call(functools.partial(main_kernel, count), out_shape=(out, out...  16.4 us
    ppermute x1, starting transfers between devices, per_device(): odd_k = lax.ppermute(k_odd, 'tm', odd_pairs)  12.2 us
    all_to_all x1, starting transfers between devices, per_device(): lax.all_to_all(out_grad, 'head', split_axis=1, concat_axis=0, tiled=True)  10.5 us
    ppermute x1, starting transfers between devices, per_device(): godd = lax.ppermute(godd, 'tm', odd_pairs)  7.9 us
    ppermute x1, waiting for transfers between devices, per_device(): godd = lax.ppermute(godd, 'tm', odd_pairs)  5.96 us
    unnamed x16, local copies, waits for them, and re-layouts  4.25 us
    pallas_call x1, Pallas kernels, stats_call(): pl.pallas_call(functools.partial(stats_kernel, count), out_shape=(out, ou...  4.21 us
    ppermute x1, starting transfers between devices, per_device(): geven = lax.ppermute(geven, 'tm', even_pairs)  4 us
  transfers between devices with their start and end apart: 9, of which 2 were waited for; matrix products, arithmetic and copies ran while one was open for 3% of the time, Pallas kernels for 5%

profile of v1, /device:TPU:58, one launch (start us, length us, event | category | flops | bytes accessed | tf_op | source)
XLA Modules:
  0.0 82.5 jit_solution(12625399012886616517)
XLA Ops:
  0.6 0.0 copy-start
  0.6 1.0 %copy-done = bf16[64,4096]{1,0:T(8,128)(2,1)S(1)} copy-done((bf16[64,4096]{1,0:T(8,128)(2,1)S(1)}, bf16[64,4096]{1,0:T(8,128)(2,1)}, u32[]{:S(2)}) %copy-start) | copy-done | bytes 524312
  1.7 0.9 %copy_bitcast_fusion = bf16[64,32,128]{2,0,1:T(8,128)(2,1)} fusion(bf16[64,4096]{1,0:T(8,128)(2,1)S(1)} %copy-done), kind=kLoop, calls=%fused_computation | loop fusion | bytes 1048576 | tf_op jit(solution)/shard_map/all_to_all | solution.py:313
  2.6 10.5 %all-to-all-start = ((bf16[64,32,128]{2,0,1:T(8,128)(2,1)}), bf16[64,32,128]{2,0,1:T(8,128)(2,1)S(1)}, u32[]{:S(2)}, u32[]{:S(2)}) async-start(bf16[64,32,128]{2,0,1:T(8,128)(2,1)} %copy_bitcast_fusion), calls=%async_computation | async-start | bytes 1048576 | tf_op jit(solution)/shard_map/all_to_all | solution.py:313
  13.3 0.9 %copy-done.3 = bf16[2048,128]{1,0:T(8,128)(2,1)S(1)} copy-done((bf16[2048,128]{1,0:T(8,128)(2,1)S(1)}, bf16[2048,128]{1,0:T(8,128)(2,1)}, u32[]{:S(2)}) %copy-start.3) | copy-done | bytes 524312
  14.2 0.1 copy-done.4
  14.5 3.3 %collective-permute-start.2 = (bf16[2048,128]{1,0:T(8,128)(2,1)S(1)}, bf16[2048,128]{1,0:T(8,128)(2,1)S(1)}, u32[]{:S(2)}, u32[]{:S(2)}) collective-permute-start(bf16[2048,128]{1,0:T(8,128)(2,1)S(1)} %pad_maximum_fusion), channel_id=1, source_target_pairs={{0,32},{64,96},{128,160},{192,224},{256,288},{320,352},{384,416},{... | collective-permute-start | bytes 1572872 | tf_op jit(solution)/shard_map/ppermute | solution.py:316
  17.7 0.7 collective-permute-start.1
  18.4 3.0 %collective-permute-start.3 = (bf16[512,128]{1,0:T(8,128)(2,1)S(1)}, bf16[512,128]{1,0:T(8,128)(2,1)S(1)}, u32[]{:S(2)}, u32[]{:S(2)}) collective-permute-start(bf16[512,128]{1,0:T(8,128)(2,1)S(1)} %get-tuple-element.10), channel_id=1, source_target_pairs={{224,0},{256,480},{480,256},{512,736},{225,1},{257,481},{481,257},... | collective-permute-start | bytes 393224 | tf_op jit(solution)/shard_map/ppermute | solution.py:315
  21.4 12.2 %collective-permute-start = (bf16[512,128]{1,0:T(8,128)(2,1)S(1)}, bf16[512,128]{1,0:T(8,128)(2,1)S(1)}, u32[]{:S(2)}, u32[]{:S(2)}) collective-permute-start(bf16[512,128]{1,0:T(8,128)(2,1)S(1)} %get-tuple-element.8), channel_id=1, source_target_pairs={{32,64},{96,128},{160,192},{224,256},{288,320},{352,384},{416,448}... | collective-permute-start | bytes 393224 | tf_op jit(solution)/shard_map/ppermute | solution.py:317
  34.3 0.6 pad_add_fusion.where_ref
  34.9 1.3 %collective-permute-start.4 = (bf16[512,128]{1,0:T(8,128)(2,1)S(1)}, bf16[512,128]{1,0:T(8,128)(2,1)S(1)}, u32[]{:S(2)}, u32[]{:S(2)}) collective-permute-start(bf16[512,128]{1,0:T(8,128)(2,1)S(1)} %collective-permute-done.3), channel_id=1, source_target_pairs={{0,256},{480,224},{256,512},{736,480},{1,257},{481,225},{257,513},... | collective-permute-start | bytes 393224 | tf_op jit(solution)/shard_map/ppermute | solution.py:319
  36.2 1.3 %collective-permute-start.5 = (bf16[512,128]{1,0:T(8,128)(2,1)S(1)}, bf16[512,128]{1,0:T(8,128)(2,1)S(1)}, u32[]{:S(2)}, u32[]{:S(2)}) collective-permute-start(bf16[512,128]{1,0:T(8,128)(2,1)S(1)} %slice.4), channel_id=1, source_target_pairs={{192,256},{288,224},{448,512},{544,480},{193,257},{289,225},{449,5... | collective-permute-start | bytes 393224 | tf_op jit(solution)/shard_map/ppermute | solution.py:320
  37.5 0.8 copy-done.1
  38.3 4.2 %rim_stats.1 = (bf16[560,128]{1,0:T(8,128)(2,1)}, bf16[560,128]{1,0:T(8,128)(2,1)}) custom-call(s32[2]{0:T(128)} %pad_add_fusion.where_ref, s32[1]{0:T(128)S(6)} %copy.12.radius_ref, s32[192]{0:T(256)} %clip_ref.3, bf16[2048,128]{1,0:T(8,128)(2,1)} %q_ref.3, bf16[2048,128]{1,0:T(8,128)(2,1)} %k_ref.3, bf16[2048,128]{1,0:T(8,128)(2,1)} %v_ref.3, ...), custom_call_target="tpu_custom_call" | custom-call | flops 536870912 | bytes 1310720 | tf_op jit(solution)/shard_map/rim_stats/pallas_call | solution.py:240
  42.5 7.9 %collective-permute-start.6 = (bf16[560,128]{1,0:T(8,128)(2,1)}, bf16[560,128]{1,0:T(8,128)(2,1)S(1)}, u32[]{:S(2)}, u32[]{:S(2)}) collective-permute-start(bf16[560,128]{1,0:T(8,128)(2,1)} %get-tuple-element.5), channel_id=1, source_target_pairs={{32,64},{96,128},{160,192},{224,256},{288,320},{352,384},{416,448}... | collective-permute-start | bytes 430088 | tf_op jit(solution)/shard_map/ppermute | solution.py:324
  50.5 4.0 %collective-permute-start.7 = (bf16[560,128]{1,0:T(8,128)(2,1)}, bf16[560,128]{1,0:T(8,128)(2,1)S(1)}, u32[]{:S(2)}, u32[]{:S(2)}) collective-permute-start(bf16[560,128]{1,0:T(8,128)(2,1)} %get-tuple-element.6), channel_id=1, source_target_pairs={{0,32},{64,96},{128,160},{192,224},{256,288},{320,352},{384,416},{... | collective-permute-start | bytes 430088 | tf_op jit(solution)/shard_map/ppermute | solution.py:325
  54.5 0.8 pad_maximum_fusion.1.odd_ref
  55.3 2.9 %collective-permute-done.5 = bf16[512,128]{1,0:T(8,128)(2,1)S(1)} collective-permute-done((bf16[512,128]{1,0:T(8,128)(2,1)S(1)}, bf16[512,128]{1,0:T(8,128)(2,1)S(1)}, u32[]{:S(2)}, u32[]{:S(2)}) %collective-permute-start.5) | collective-permute-done | bytes 131104 | tf_op jit(solution)/shard_map/ppermute | solution.py:320
  58.1 0.7 pad_maximum_fusion.3.relay_ref
  58.9 6.0 %collective-permute-done.6.godd_ref = bf16[560,128]{1,0:T(8,128)(2,1)S(1)} collective-permute-done((bf16[560,128]{1,0:T(8,128)(2,1)}, bf16[560,128]{1,0:T(8,128)(2,1)S(1)}, u32[]{:S(2)}, u32[]{:S(2)}) %collective-permute-start.6) | collective-permute-done | bytes 143392 | tf_op jit(solution)/shard_map/ppermute | solution.py:324
  64.8 0.6 copy-done.6
  65.5 0.6 copy-done.7
  66.1 16.4 %band_grads.1 = (bf16[2048,128]{1,0:T(8,128)(2,1)}, bf16[2048,128]{1,0:T(8,128)(2,1)}, bf16[2048,128]{1,0:T(8,128)(2,1)}) custom-call(s32[2]{0:T(128)} %pad_add_fusion.where_ref, s32[1]{0:T(128)S(6)} %copy.12.radius_ref, s32[192]{0:T(256)} %clip_ref.3, bf16[2048,128]{1,0:T(8,128)(2,1)} %q_ref.3, bf16[2048,128]{1,0:T(8,128)(2,1)} %k_ref.3, ...), custom_call_target="tpu_custom_call" | custom-call | flops 3858759680 | bytes 3670016 | tf_op jit(solution)/shard_map/band_grads/pallas_call | solution.py:259
  (22 shorter events, 0.2 us)
Async XLA Ops:
  0.6 1.0 %copy-start = (bf16[64,4096]{1,0:T(8,128)(2,1)S(1)}, bf16[64,4096]{1,0:T(8,128)(2,1)}, u32[]{:S(2)}) copy-start(bf16[64,4096]{1,0:T(8,128)(2,1)} %param.9) | copy-start | bytes 1572868
  2.6 10.6 %copy-start.2 = (bf16[2048,128]{1,0:T(8,128)(2,1)S(1)}, bf16[2048,128]{1,0:T(8,128)(2,1)}, u32[]{:S(2)}) copy-start(bf16[2048,128]{1,0:T(8,128)(2,1)} %q_ref.3) | copy-start | bytes 1572868
  2.6 34.9 %all-to-all-start = ((bf16[64,32,128]{2,0,1:T(8,128)(2,1)}), bf16[64,32,128]{2,0,1:T(8,128)(2,1)S(1)}, u32[]{:S(2)}, u32[]{:S(2)}) async-start(bf16[64,32,128]{2,0,1:T(8,128)(2,1)} %copy_bitcast_fusion), calls=%async_computation | async-start | bytes 1048576 | tf_op jit(solution)/shard_map/all_to_all | solution.py:313
  13.2 1.0 %copy-start.3 = (bf16[2048,128]{1,0:T(8,128)(2,1)S(1)}, bf16[2048,128]{1,0:T(8,128)(2,1)}, u32[]{:S(2)}) copy-start(bf16[2048,128]{1,0:T(8,128)(2,1)} %k_ref.3) | copy-start | bytes 1572868
  13.2 1.2 %copy-start.4 = (bf16[2048,128]{1,0:T(8,128)(2,1)S(1)}, bf16[2048,128]{1,0:T(8,128)(2,1)}, u32[]{:S(2)}) copy-start(bf16[2048,128]{1,0:T(8,128)(2,1)} %v_ref.3) | copy-start | bytes 1572868
  14.5 21.7 %collective-permute-start.2 = (bf16[2048,128]{1,0:T(8,128)(2,1)S(1)}, bf16[2048,128]{1,0:T(8,128)(2,1)S(1)}, u32[]{:S(2)}, u32[]{:S(2)}) collective-permute-start(bf16[2048,128]{1,0:T(8,128)(2,1)S(1)} %pad_maximum_fusion), channel_id=1, source_target_pairs={{0,32},{64,96},{128,160},{192,224},{256,288},{320,352},{384,416},{... | collective-permute-start | bytes 1572872 | tf_op jit(solution)/shard_map/ppermute | solution.py:316
  17.7 36.7 %collective-permute-start.1 = (bf16[1024,128]{1,0:T(8,128)(2,1)S(1)}, bf16[1024,128]{1,0:T(8,128)(2,1)S(1)}, u32[]{:S(2)}, u32[]{:S(2)}) collective-permute-start(bf16[1024,128]{1,0:T(8,128)(2,1)S(1)} %pad_maximum_fusion.2), channel_id=1, source_target_pairs={{32,64},{96,128},{160,192},{288,320},{352,384},{416,448},{544,576}... | collective-permute-start | bytes 786440 | tf_op jit(solution)/shard_map/ppermute | solution.py:318
  18.4 16.5 %collective-permute-start.3 = (bf16[512,128]{1,0:T(8,128)(2,1)S(1)}, bf16[512,128]{1,0:T(8,128)(2,1)S(1)}, u32[]{:S(2)}, u32[]{:S(2)}) collective-permute-start(bf16[512,128]{1,0:T(8,128)(2,1)S(1)} %get-tuple-element.10), channel_id=1, source_target_pairs={{224,0},{256,480},{480,256},{512,736},{225,1},{257,481},{481,257},... | collective-permute-start | bytes 393224 | tf_op jit(solution)/shard_map/ppermute | solution.py:315
  21.4 29.0 %collective-permute-start = (bf16[512,128]{1,0:T(8,128)(2,1)S(1)}, bf16[512,128]{1,0:T(8,128)(2,1)S(1)}, u32[]{:S(2)}, u32[]{:S(2)}) collective-permute-start(bf16[512,128]{1,0:T(8,128)(2,1)S(1)} %get-tuple-element.8), channel_id=1, source_target_pairs={{32,64},{96,128},{160,192},{224,256},{288,320},{352,384},{416,448}... | collective-permute-start | bytes 393224 | tf_op jit(solution)/shard_map/ppermute | solution.py:317
  34.9 20.4 %collective-permute-start.4 = (bf16[512,128]{1,0:T(8,128)(2,1)S(1)}, bf16[512,128]{1,0:T(8,128)(2,1)S(1)}, u32[]{:S(2)}, u32[]{:S(2)}) collective-permute-start(bf16[512,128]{1,0:T(8,128)(2,1)S(1)} %collective-permute-done.3), channel_id=1, source_target_pairs={{0,256},{480,224},{256,512},{736,480},{1,257},{481,225},{257,513},... | collective-permute-start | bytes 393224 | tf_op jit(solution)/shard_map/ppermute | solution.py:319
  36.2 19.1 %copy-start.5 = (bf16[2048,128]{1,0:T(8,128)(2,1)}, bf16[2048,128]{1,0:T(8,128)(2,1)S(1)}, u32[]{:S(2)}) copy-start(bf16[2048,128]{1,0:T(8,128)(2,1)S(1)} %collective-permute-done.2.even_ref) | copy-start | bytes 1572868
  36.2 21.9 %collective-permute-start.5 = (bf16[512,128]{1,0:T(8,128)(2,1)S(1)}, bf16[512,128]{1,0:T(8,128)(2,1)S(1)}, u32[]{:S(2)}, u32[]{:S(2)}) collective-permute-start(bf16[512,128]{1,0:T(8,128)(2,1)S(1)} %slice.4), channel_id=1, source_target_pairs={{192,256},{288,224},{448,512},{544,480},{193,257},{289,225},{449,5... | collective-permute-start | bytes 393224 | tf_op jit(solution)/shard_map/ppermute | solution.py:320
  37.5 0.8 copy-start.1
  42.5 22.3 %collective-permute-start.6 = (bf16[560,128]{1,0:T(8,128)(2,1)}, bf16[560,128]{1,0:T(8,128)(2,1)S(1)}, u32[]{:S(2)}, u32[]{:S(2)}) collective-permute-start(bf16[560,128]{1,0:T(8,128)(2,1)} %get-tuple-element.5), channel_id=1, source_target_pairs={{32,64},{96,128},{160,192},{224,256},{288,320},{352,384},{416,448}... | collective-permute-start | bytes 430088 | tf_op jit(solution)/shard_map/ppermute | solution.py:324
  50.5 14.4 %collective-permute-start.7 = (bf16[560,128]{1,0:T(8,128)(2,1)}, bf16[560,128]{1,0:T(8,128)(2,1)S(1)}, u32[]{:S(2)}, u32[]{:S(2)}) collective-permute-start(bf16[560,128]{1,0:T(8,128)(2,1)} %get-tuple-element.6), channel_id=1, source_target_pairs={{0,32},{64,96},{128,160},{192,224},{256,288},{320,352},{384,416},{... | collective-permute-start | bytes 430088 | tf_op jit(solution)/shard_map/ppermute | solution.py:325
  64.8 0.7 copy-start.6
  65.5 0.6 copy-start.7

commit v2 on v1

v2 whole, which is shorter than its diff:
```python
import functools

import jax
import jax.numpy as jnp
from jax import lax
from jax.experimental import pallas as pl
from jax.experimental.pallas import tpu as pltpu
from jax.sharding import PartitionSpec as P


FRAME = 256
RADIUS = 2
SPAN = 2 * RADIUS + 1
NEG = -1e30
LOG2E = 1.4426950408889634
STAT_ROWS = 48
STATS_VMEM, OWN_VMEM, RIM_VMEM = 16, 32, 16

NT = (((1,), (1,)), ((), ()))
NN = (((1,), (0,)), ((), ()))


def dot(a, b, dims):
    return lax.dot_general(a, b, dims, preferred_element_type=jnp.float32)


def make_allowed(where_ref, radius_ref, clip_ref, count):
    first = where_ref[0] * count
    total = clip_ref.shape[0]
    radius = radius_ref[0]

    def allowed(query, key):
        fq = first + query
        fk = first + key
        inside = (fq >= 0) & (fq < total) & (fk >= 0) & (fk < total)
        cq = clip_ref[jnp.clip(fq, 0, total - 1)]
        ck = clip_ref[jnp.clip(fk, 0, total - 1)]
        return inside & (abs(query - key) <= radius) & (cq == ck)

    return allowed


def block(ref, index):
    return ref[index * FRAME : (index + 1) * FRAME, :]


def raw_scores(keys, q, s_scr, valid, top):
    for n, key in enumerate(keys):
        s = dot(key, q, NT)
        s_scr[n] = s
        peak = jnp.where(valid[n], jnp.max(s, axis=0, keepdims=True), NEG)
        top = peak if top is None else jnp.maximum(top, peak)
    return top


def exponentials(values, g, s_scr, dp_scr, valid, top, total, delta, c, keep):
    for n, value in enumerate(values):
        shift = jnp.where(valid[n], top, -NEG)
        e = jnp.exp2((s_scr[n] - shift) * c)
        dp = dot(value, g, NT)
        total = total + jnp.sum(e, axis=0, keepdims=True)
        delta = delta + jnp.sum(e * dp, axis=0, keepdims=True)
        if keep:
            s_scr[n] = e
            dp_scr[n] = dp
    return total, delta


def stats_kernel(count, where_ref, radius_ref, clip_ref, q_ref, k_ref, v_ref, g_ref, odd_ref, even_ref, s_scr, row_scr, out_scr):
    c = q_ref.shape[1] ** -0.5 * LOG2E
    allowed = make_allowed(where_ref, radius_ref, clip_ref, count)
    parity = lax.rem(where_ref[0], 2)
    row_scr[...] = jnp.zeros_like(row_scr)
    jobs = []
    for side in range(2):
        for i in range(RADIUS):
            qf = side * (count - RADIUS) + i
            keys = [f for f in range(qf - RADIUS, qf + RADIUS + 1) if 0 <= f < count]
            jobs.append((side, i, qf, keys))
    tops = {}

    def begin(n):
        _, _, qf, keys = jobs[n]
        valid = [allowed(qf, f) for f in keys]
        top = raw_scores([block(k_ref, f) for f in keys], block(q_ref, qf), s_scr.at[n], valid, None)
        tops[n] = (valid, top)

    def finish(n):
        side, i, qf, keys = jobs[n]
        valid, top = tops[n]
        zero = jnp.zeros_like(top)
        g = block(g_ref, qf)
        out_scr[side, i * FRAME : (i + 1) * FRAME, :] = g
        total, delta = exponentials([block(v_ref, f) for f in keys], g, s_scr.at[n], None, valid, top, zero, zero, c, False)
        row = side * STAT_ROWS + i * 18
        for stat in (top, total, delta):
            rest = stat
            for _ in range(3):
                part = rest.astype(jnp.bfloat16).astype(jnp.float32)
                rest = rest - part
                row_scr[row : row + 1, :] = part[:, :128]
                row_scr[row + 1 : row + 2, :] = part[:, 128:]
                row += 2

    begin(0)
    for n in range(len(jobs)):
        if n + 1 < len(jobs):
            begin(n + 1)
        finish(n)
    for side in range(2):
        out_scr[side, RADIUS * FRAME :, :] = row_scr[side * STAT_ROWS : (side + 1) * STAT_ROWS, :].astype(jnp.bfloat16)
    odd_ref[...] = out_scr[parity]
    even_ref[...] = out_scr[1 - parity]


def own_kernel(
    count,
    where_ref,
    radius_ref,
    clip_ref,
    q_ref,
    k_ref,
    v_ref,
    g_ref,
    kodd_ref,
    vodd_ref,
    vrelay_ref,
    keven_ref,
    veven_ref,
    dq_ref,
    dk_ref,
    dv_ref,
    dk_part,
    dv_part,
    kx,
    vx,
    kt,
    dk_acc,
    dv_acc,
    s_scr,
    dp_scr,
):
    scale = q_ref.shape[1] ** -0.5
    c = scale * LOG2E
    allowed = make_allowed(where_ref, radius_ref, clip_ref, count)
    parity = lax.rem(where_ref[0], 2)
    kx[parity] = kodd_ref[...]
    vx[parity] = vodd_ref[...]
    kx[1 - parity] = keven_ref[...]
    vx[1 - parity] = veven_ref[...]

    @pl.when(where_ref[1] == 1)
    def _():
        vx[parity] = vrelay_ref[...]

    def frame_of(own_ref, halo, f):
        if 0 <= f < count:
            return block(own_ref, f)
        side, i = (0, f + RADIUS) if f < 0 else (1, f - count)
        return halo[side, i * FRAME : (i + 1) * FRAME, :]

    def turn(f):
        kt[:, (f + RADIUS) * FRAME : (f + RADIUS + 1) * FRAME] = frame_of(k_ref, kx, f).T

    tops = {}

    def begin(a):
        keys = range(a - RADIUS, a + RADIUS + 1)
        valid = [True if f == a else allowed(a, f) for f in keys]
        top = raw_scores([frame_of(k_ref, kx, f) for f in keys], block(q_ref, a), s_scr.at[a % 2], valid, None)
        tops[a] = (valid, top)

    begin(0)
    for f in range(-RADIUS, RADIUS):
        turn(f)
    for a in range(count):
        if a + 1 < count:
            begin(a + 1)
        turn(a + RADIUS)
        keys = list(range(a - RADIUS, a + RADIUS + 1))
        valid, top = tops[a]
        q = block(q_ref, a)
        g = block(g_ref, a)
        zero = jnp.zeros_like(top)
        s_a, dp_a = s_scr.at[a % 2], dp_scr.at[a % 2]
        total, delta = exponentials([frame_of(v_ref, vx, f) for f in keys], g, s_a, dp_a, valid, top, zero, zero, c, True)
        inverse = 1.0 / total
        delta = delta * inverse
        dqt = None
        for n, f in enumerate(keys):
            p = s_a[n] * inverse
            ds = (p * (dp_a[n] - delta)).astype(jnp.bfloat16)
            part = dot(kt[:, (f + RADIUS) * FRAME : (f + RADIUS + 1) * FRAME], ds, NN)
            dqt = part if dqt is None else dqt + part
            if not 0 <= f < count:
                continue
            dv = dot(p.astype(jnp.bfloat16), g, NN)
            dk = dot(ds, q, NN)
            rows = slice(f * FRAME, (f + 1) * FRAME)
            if a > max(0, f - RADIUS):
                dv = dv + dv_acc[rows, :]
                dk = dk + dk_acc[rows, :]
            if a < min(count - 1, f + RADIUS):
                dv_acc[rows, :] = dv
                dk_acc[rows, :] = dk
            elif RADIUS <= f < count - RADIUS:
                dv_ref[rows, :] = dv.astype(jnp.bfloat16)
                dk_ref[rows, :] = (dk * scale).astype(jnp.bfloat16)
            else:
                at = f if f < RADIUS else f - count + 2 * RADIUS
                part_rows = slice(at * FRAME, (at + 1) * FRAME)
                dv_part[part_rows, :] = dv
                dk_part[part_rows, :] = dk
                dv_ref[rows, :] = dv.astype(jnp.bfloat16)
                dk_ref[rows, :] = dk.astype(jnp.bfloat16)
        dq_ref[a * FRAME : (a + 1) * FRAME, :] = (dqt * scale).T.astype(jnp.bfloat16)


def rim_kernel(
    count,
    where_ref,
    radius_ref,
    clip_ref,
    k_ref,
    v_ref,
    dk_part,
    dv_part,
    qodd_ref,
    qrelay_ref,
    qeven_ref,
    godd_ref,
    geven_ref,
    dk_in,
    dv_in,
    dk_ref,
    dv_ref,
    qx,
    gx,
    s_scr,
    dp_scr,
):
    scale = k_ref.shape[1] ** -0.5
    c = scale * LOG2E
    rim = RADIUS * FRAME
    allowed = make_allowed(where_ref, radius_ref, clip_ref, count)
    parity = lax.rem(where_ref[0], 2)
    side_now = pl.program_id(0)

    @pl.when(parity == side_now)
    def _():
        qx[...] = qodd_ref[...]
        gx[...] = godd_ref[...]

    @pl.when((parity == side_now) & (where_ref[1] == 1))
    def _():
        qx[...] = qrelay_ref[...]

    @pl.when(parity != side_now)
    def _():
        qx[...] = qeven_ref[...]
        gx[...] = geven_ref[...]

    def one_side(side):
        stat = gx[rim:, :].astype(jnp.float32)
        sums = [None] * RADIUS
        state = {}
        for i in range(RADIUS):
            qf = i - RADIUS if side == 0 else count + i
            slots = list(range(0, i + 1)) if side == 0 else list(range(i, RADIUS))
            frames = slots if side == 0 else [f + count - RADIUS for f in slots]
            stats = []
            row = i * 18
            for _ in range(3):
                halves = [stat[row + n : row + n + 1] + stat[row + 2 + n : row + 3 + n] + stat[row + 4 + n : row + 5 + n] for n in range(2)]
                stats.append(jnp.concatenate(halves, axis=1))
                row += 6
            valid = [allowed(qf, f) for f in frames]
            top = raw_scores([block(k_ref, n) for n in slots], block(qx, i), s_scr.at[i], valid, stats[0])
            state[i] = (slots, valid, stats, top)
        for i in range(RADIUS):
            slots, valid, (far_top, total, delta), top = state[i]
            q, g = block(qx, i), block(gx, i)
            s_i, dp_i = s_scr.at[i], dp_scr.at[i]
            fade = jnp.exp2((far_top - top) * c)
            total, delta = exponentials([block(v_ref, n) for n in slots], g, s_i, dp_i, valid, top, total * fade, delta * fade, c, True)
            inverse = jnp.where(total > 0.0, 1.0 / total, 0.0)
            delta = delta * inverse
            for n, slot in enumerate(slots):
                p = s_i[n] * inverse
                ds = (p * (dp_i[n] - delta)).astype(jnp.bfloat16)
                dv = dot(p.astype(jnp.bfloat16), g, NN)
                dk = dot(ds, q, NN)
                old = sums[slot]
                sums[slot] = (dv, dk) if old is None else (old[0] + dv, old[1] + dk)
        for slot in range(RADIUS):
            rows = slice(slot * FRAME, (slot + 1) * FRAME)
            dv_ref[rows, :] = (dv_part[rows, :] + sums[slot][0]).astype(jnp.bfloat16)
            dk_ref[rows, :] = ((dk_part[rows, :] + sums[slot][1]) * scale).astype(jnp.bfloat16)

    for side in range(2):
        pl.when(side_now == side)(functools.partial(one_side, side))


VM = pl.BlockSpec(memory_space=pltpu.VMEM)
SM = pl.BlockSpec(memory_space=pltpu.SMEM)
MIB = 1 << 20


def piece(rows, width, index):
    return pl.BlockSpec((rows, width), lambda i: (index, 0))


def stats_call(scalars, q, k, v, g):
    rows, width = q.shape
    count = rows // FRAME
    out = jax.ShapeDtypeStruct((RADIUS * FRAME + STAT_ROWS, width), jnp.bfloat16)
    return pl.pallas_call(
        functools.partial(stats_kernel, count),
        out_shape=(out, out),
        in_specs=[SM] * 3 + [VM] * 4,
        out_specs=(VM, VM),
        scratch_shapes=[
            pltpu.VMEM((2 * RADIUS, 2 * RADIUS, FRAME, FRAME), jnp.float32),
            pltpu.VMEM((2 * STAT_ROWS, width), jnp.float32),
            pltpu.VMEM((2, RADIUS * FRAME + STAT_ROWS, width), jnp.bfloat16),
        ],
        compiler_params=pltpu.CompilerParams(vmem_limit_bytes=STATS_VMEM * MIB),
        cost_estimate=pl.CostEstimate(flops=14 * 4 * FRAME * FRAME * width, bytes_accessed=5 * rows * width, transcendentals=0),
        name="rim_stats",
    )(*scalars, q, k, v, g)


def own_call(scalars, q, k, v, g, kodd, vqodd, vrelay, even):
    rows, width = q.shape
    count = rows // FRAME
    rim = RADIUS * FRAME
    out = jax.ShapeDtypeStruct((rows, width), jnp.bfloat16)
    part = jax.ShapeDtypeStruct((2 * rim, width), jnp.float32)
    whole = piece(rows, width, 0)
    half = piece(rim, width, 0)
    return pl.pallas_call(
        functools.partial(own_kernel, count),
        out_shape=(out, out, out, part, part),
        grid=(1,),
        in_specs=[SM] * 3 + [whole] * 4 + [half, half, half, half, piece(rim, width, 1)],
        out_specs=(whole, whole, whole, piece(2 * rim, width, 0), piece(2 * rim, width, 0)),
        scratch_shapes=[
            pltpu.VMEM((2, rim, width), jnp.bfloat16),
            pltpu.VMEM((2, rim, width), jnp.bfloat16),
            pltpu.VMEM((width, rows + 2 * rim), jnp.bfloat16),
            pltpu.VMEM((rows, width), jnp.float32),
            pltpu.VMEM((rows, width), jnp.float32),
            pltpu.VMEM((2, SPAN, FRAME, FRAME), jnp.float32),
            pltpu.VMEM((2, SPAN, FRAME, FRAME), jnp.float32),
        ],
        compiler_params=pltpu.CompilerParams(vmem_limit_bytes=OWN_VMEM * MIB),
        cost_estimate=pl.CostEstimate(flops=40 * 10 * FRAME * FRAME * width, bytes_accessed=14 * rows * width, transcendentals=0),
        name="own_rows",
    )(*scalars, q, k, v, g, kodd, vqodd, vrelay, even, even)


def rim_call(scalars, k, v, dk_part, dv_part, vqodd, qrelay, even, godd, geven, dk, dv):
    rows, width = k.shape
    count = rows // FRAME
    rim = RADIUS * FRAME
    out = jax.ShapeDtypeStruct((rows, width), jnp.bfloat16)
    edge = pl.BlockSpec((rim, width), lambda i: (i * (count // RADIUS - 1), 0))
    part = pl.BlockSpec((rim, width), lambda i: (i, 0))
    grads = piece(rim + STAT_ROWS, width, 0)
    untouched = pl.BlockSpec(memory_space=pl.ANY)
    return pl.pallas_call(
        functools.partial(rim_kernel, count),
        out_shape=(out, out),
        grid=(2,),
        in_specs=[SM] * 3
        + [edge, edge, part, part, piece(rim, width, 1), piece(rim, width, 0), piece(rim, width, 2), grads, grads]
        + [untouched] * 2,
        out_specs=(edge, edge),
        input_output_aliases={12: 0, 13: 1},
        scratch_shapes=[
            pltpu.VMEM((rim, width), jnp.bfloat16),
            pltpu.VMEM((rim + STAT_ROWS, width), jnp.bfloat16),
            pltpu.VMEM((RADIUS, RADIUS, FRAME, FRAME), jnp.float32),
            pltpu.VMEM((RADIUS, RADIUS, FRAME, FRAME), jnp.float32),
        ],
        compiler_params=pltpu.CompilerParams(vmem_limit_bytes=RIM_VMEM * MIB),
        cost_estimate=pl.CostEstimate(flops=6 * 8 * FRAME * FRAME * width, bytes_accessed=6 * rows * width, transcendentals=0),
        name="rim_rows",
    )(*scalars, k, v, dk_part, dv_part, vqodd, qrelay, even, godd, geven, dk, dv)


def both_ways(pairs):
    return pairs + [(b, a) for a, b in pairs]


def exchange_pairs(size, plane):
    odd = both_ways([(i, i + 1) for i in range(1, size - 1, 2)])
    even = both_ways([(i, i + 1) for i in range(0, size - 1, 2)])
    far = [(i, i + 1) for i in range(plane - 1, size - 1, plane)]
    near_odd = [p for p in odd if p not in both_ways(far)]
    first, second, third = [], [], []
    for a, b in far:
        low, high = a - plane + 1, b + plane - 1
        first += [(a, low), (b, high)]
        second += [(low, b), (high, a)]
        third += [(a - 1, b), (b + 1, a)]
    return odd, near_odd, even, far, first, second, third


def per_device(queries, saved_keys, saved_values, out_grad, radius, clip_ids):
    size = lax.axis_size("tm")
    tm = lax.axis_index("tm")
    rows = queries.shape[0]
    rim = RADIUS * FRAME
    parity = tm % 2
    odd_pairs, near_pairs, even_pairs, far_pairs, hop_a1, hop_a2, hop_b2 = exchange_pairs(size, 8)
    is_far = sum((tm == i).astype(jnp.int32) for pair in far_pairs for i in pair)
    where = jnp.stack([tm.astype(jnp.int32), is_far])

    def rim_of(x, slot):
        last = parity if slot == 0 else 1 - parity
        return lax.dynamic_slice_in_dim(x, last * (rows - rim), rim, 0)

    grads = lax.all_to_all(out_grad, "head", split_axis=1, concat_axis=0, tiled=True)
    k_odd, v_odd, q_odd = (rim_of(x, 0) for x in (saved_keys, saved_values, queries))
    relay_v = lax.ppermute(v_odd, "tm", hop_a1)
    even = lax.ppermute(jnp.concatenate([rim_of(x, 1) for x in (saved_keys, saved_values, queries)] + [q_odd], 0), "tm", even_pairs)
    odd_k = lax.ppermute(k_odd, "tm", odd_pairs)
    odd_vq = lax.ppermute(jnp.concatenate([v_odd, q_odd], 0), "tm", near_pairs)
    relay_v = lax.ppermute(relay_v, "tm", hop_a2)
    relay_q = lax.ppermute(even[3 * rim :], "tm", hop_b2)
    scalars = (where, radius, clip_ids)
    godd, geven = stats_call(scalars, queries, saved_keys, saved_values, grads)
    godd = lax.ppermute(godd, "tm", odd_pairs)
    geven = lax.ppermute(geven, "tm", even_pairs)
    dq, dk, dv, dk_part, dv_part = own_call(scalars, queries, saved_keys, saved_values, grads, odd_k, odd_vq, relay_v, even)
    dk, dv = rim_call(scalars, saved_keys, saved_values, dk_part, dv_part, odd_vq, relay_q, even, godd, geven, dk, dv)
    return dq, dk, dv


def solution(mesh):
    placed = (P("tm", "head"),) * 3 + (P(("tm", "head"), None), P("head"), P())
    return jax.shard_map(
        per_device,
        mesh=mesh,
        in_specs=placed,
        out_specs=(P("tm", "head"),) * 3,
        check_vma=False,
    )
```

time: 83 us -> 70.6 us (0.85)
  waiting for transfers between devices: 8.83 us -> 1.93 us
  Pallas kernels: 20.6 us -> 16.9 us
  local copies, waits for them, and re-layouts: 5.26 us -> 3.86 us
    ppermute x1, waiting for transfers between devices: 5.96 us -> 0.01 us  [per_device(): godd = lax.ppermute(godd, 'tm', odd_pairs)]
    ppermute x1, waiting for transfers between devices: 2.86 us -> 0.01 us  [per_device(): relay_q = lax.ppermute(even[3 * rim:], 'tm', hop_b2)]
    unnamed x16 -> x10, local copies, waits for them, and re-layouts: 4.25 us -> 1.56 us
    pallas_call x1, Pallas kernels: 4.21 us -> 1.89 us  [stats_call(): pl.pallas_call(functools.partial(stats_kernel, count), out_shape=(out, ou...]
    ppermute x1, waiting for transfers between devices: 0.01 us -> 1.91 us  [per_device(): relay_v = lax.ppermute(relay_v, 'tm', hop_a2)]
    concatenate x2 -> x0, other arithmetic: 1.51 us -> none  [the longest x1 0.79 us: per_device(): odd = jnp.concatenate([odd_k, odd_vq], 0)]
    pallas_call x1 -> x2, Pallas kernels: 16.4 us -> 15 us  [the longest x1 11.8 us: own_call(): pl.pallas_call(functools.partial(own_kernel, count), out_shape=(out, out,...]
  transfers between devices with their start and end apart: 9 -> 9, of which waited for: 2 -> 1; matrix products, arithmetic and copies ran while one was open for 3% -> 4% of each run, Pallas kernels for 5% -> 20%
where the time goes in v2:
time: 70.6 us; the launch traced here: 70.1 us
  starting transfers between devices  44.3 us (63%)
  Pallas kernels  16.9 us (24%)
  local copies, waits for them, and re-layouts  3.86 us (5%)
  waiting for transfers between devices  1.93 us (3%)
  other arithmetic  1.62 us (2%)
  between operations  1.48 us (2%)
    pallas_call x1, Pallas kernels, own_call(): pl.pallas_call(functools.partial(own_kernel, count), out_shape=(out, out,...  11.8 us
    ppermute x1, starting transfers between devices, per_device(): odd_k = lax.ppermute(k_odd, 'tm', odd_pairs)  11.6 us
    all_to_all x1, starting transfers between devices, per_device(): lax.all_to_all(out_grad, 'head', split_axis=1, concat_axis=0, tiled=True)  10.5 us
    ppermute x1, starting transfers between devices, per_device(): godd = lax.ppermute(godd, 'tm', odd_pairs)  7.9 us
    ppermute x1, starting transfers between devices, per_device(): geven = lax.ppermute(geven, 'tm', even_pairs)  4 us
    ppermute x1, starting transfers between devices, per_device(): relay_v = lax.ppermute(v_odd, 'tm', hop_a1)  3.65 us
    ppermute x1, starting transfers between devices, per_device(): lax.ppermute(jnp.concatenate([rim_of(x, 1) for x in (saved_keys, saved_va...  3.24 us
    pallas_call x1, Pallas kernels, rim_call(): pl.pallas_call(functools.partial(rim_kernel, count), out_shape=(out, out)...  3.19 us
  transfers between devices with their start and end apart: 9, of which 1 were waited for; matrix products, arithmetic and copies ran while one was open for 4% of the time, Pallas kernels for 20%

profile of v2, /device:TPU:58, one launch (start us, length us, event | category | flops | bytes accessed | tf_op | source)
XLA Modules:
  0.0 70.1 jit_solution(6890741246669251859)
XLA Ops:
  0.6 0.0 copy-start
  0.6 1.0 %copy-done = bf16[64,4096]{1,0:T(8,128)(2,1)S(1)} copy-done((bf16[64,4096]{1,0:T(8,128)(2,1)S(1)}, bf16[64,4096]{1,0:T(8,128)(2,1)}, u32[]{:S(2)}) %copy-start) | copy-done | bytes 524312
  1.7 0.9 %copy_bitcast_fusion = bf16[64,32,128]{2,0,1:T(8,128)(2,1)} fusion(bf16[64,4096]{1,0:T(8,128)(2,1)S(1)} %copy-done), kind=kLoop, calls=%fused_computation | loop fusion | bytes 1048576 | tf_op jit(solution)/shard_map/all_to_all | solution.py:424
  2.6 10.5 %all-to-all-start = ((bf16[64,32,128]{2,0,1:T(8,128)(2,1)}), bf16[64,32,128]{2,0,1:T(8,128)(2,1)S(1)}, u32[]{:S(2)}, u32[]{:S(2)}) async-start(bf16[64,32,128]{2,0,1:T(8,128)(2,1)} %copy_bitcast_fusion), calls=%async_computation | async-start | bytes 1048576 | tf_op jit(solution)/shard_map/all_to_all | solution.py:424
  13.2 0.0 copy-start.3
  13.2 0.7 constant_dynamic-slice_fusion.2
  13.9 0.4 copy-done.3
  14.3 0.1 copy-done.2
  14.5 0.8 %pad_maximum_fusion = bf16[2048,128]{1,0:T(8,128)(2,1)} fusion(bf16[512,128]{1,0:T(8,128)(2,1)S(1)} %get-tuple-element.26, bf16[512,128]{1,0:T(8,128)(2,1)S(1)} %get-tuple-element.25, bf16[512,128]{1,0:T(8,128)(2,1)S(1)} %get-tuple-element.23, bf16[512,128]{1,0:T(8,128)(2,1)S(1)} %get-tuple-element.21), kind=kLoop, calls=%fused_computation.1 | loop fusion | flops 2097152 | bytes 1048576 | tf_op jit(solution)/shard_map/concatenate | solution.py:427
  15.3 3.2 %collective-permute-start.4 = (bf16[2048,128]{1,0:T(8,128)(2,1)}, bf16[2048,128]{1,0:T(8,128)(2,1)S(1)}, u32[]{:S(2)}, u32[]{:S(2)}) collective-permute-start(bf16[2048,128]{1,0:T(8,128)(2,1)} %pad_maximum_fusion), channel_id=1, source_target_pairs={{0,32},{64,96},{128,160},{192,224},{256,288},{320,352},{384,416},{... | collective-permute-start | bytes 1572872 | tf_op jit(solution)/shard_map/ppermute | solution.py:427
  18.5 3.6 %collective-permute-start.2 = (bf16[512,128]{1,0:T(8,128)(2,1)S(1)}, bf16[512,128]{1,0:T(8,128)(2,1)}, u32[]{:S(2)}, u32[]{:S(2)}) collective-permute-start(bf16[512,128]{1,0:T(8,128)(2,1)S(1)} %get-tuple-element.24), channel_id=1, source_target_pairs={{224,0},{256,480},{480,256},{512,736},{225,1},{257,481},{481,257},... | collective-permute-start | bytes 393224 | tf_op jit(solution)/shard_map/ppermute | solution.py:426
  22.2 0.7 %pad_maximum_fusion.1 = bf16[1024,128]{1,0:T(8,128)(2,1)} fusion(bf16[512,128]{1,0:T(8,128)(2,1)S(1)} %get-tuple-element.26, bf16[512,128]{1,0:T(8,128)(2,1)S(1)} %get-tuple-element.24), kind=kLoop, calls=%fused_computation.2 | loop fusion | flops 524288 | bytes 524288 | tf_op jit(solution)/shard_map/concatenate | solution.py:429
  22.9 0.7 collective-permute-start.1
  23.6 11.6 %collective-permute-start = (bf16[512,128]{1,0:T(8,128)(2,1)}, bf16[512,128]{1,0:T(8,128)(2,1)}, u32[]{:S(2)}, u32[]{:S(2)}) collective-permute-start(bf16[512,128]{1,0:T(8,128)(2,1)} %get-tuple-element.22), channel_id=1, source_target_pairs={{32,64},{96,128},{160,192},{224,256},{288,320},{352,384},{416,448}... | collective-permute-start | bytes 393224 | tf_op jit(solution)/shard_map/ppermute | solution.py:428
  35.8 1.3 %collective-permute-start.3 = (bf16[512,128]{1,0:T(8,128)(2,1)}, bf16[512,128]{1,0:T(8,128)(2,1)}, u32[]{:S(2)}, u32[]{:S(2)}) collective-permute-start(bf16[512,128]{1,0:T(8,128)(2,1)} %collective-permute-done.2), channel_id=1, source_target_pairs={{0,256},{480,224},{256,512},{736,480},{1,257},{481,225},{257,513},... | collective-permute-start | bytes 393224 | tf_op jit(solution)/shard_map/ppermute | solution.py:430
  37.1 0.1 pad_add_fusion.where_ref
  37.2 0.7 slice.4
  37.9 1.4 %collective-permute-start.5 = (bf16[512,128]{1,0:T(8,128)(2,1)}, bf16[512,128]{1,0:T(8,128)(2,1)S(1)}, u32[]{:S(2)}, u32[]{:S(2)}) collective-permute-start(bf16[512,128]{1,0:T(8,128)(2,1)} %slice.4), channel_id=1, source_target_pairs={{192,256},{288,224},{448,512},{544,480},{193,257},{289,225},{449,5... | collective-permute-start | bytes 393224 | tf_op jit(solution)/shard_map/ppermute | solution.py:431
  39.3 1.9 %rim_stats.1 = (bf16[560,128]{1,0:T(8,128)(2,1)S(1)}, bf16[560,128]{1,0:T(8,128)(2,1)S(1)}) custom-call(s32[2]{0:T(128)S(1)} %pad_add_fusion.where_ref, s32[1]{0:T(128)S(6)} %copy.16.radius_ref, s32[192]{0:T(256)S(1)} %copy-done.4, bf16[2048,128]{1,0:T(8,128)(2,1)S(1)} %copy-done.3, bf16[2048,128]{1,0:T(8,128)(2,1)S(1)} %copy-done.1, ...), custom_call_target="tpu_custom_call" | custom-call | flops 469762048 | bytes 1310720 | tf_op jit(solution)/shard_map/rim_stats/pallas_call | solution.py:317
  41.2 7.9 %collective-permute-start.6 = (bf16[560,128]{1,0:T(8,128)(2,1)S(1)}, bf16[560,128]{1,0:T(8,128)(2,1)S(1)}, u32[]{:S(2)}, u32[]{:S(2)}) collective-permute-start(bf16[560,128]{1,0:T(8,128)(2,1)S(1)} %get-tuple-element.15), channel_id=1, source_target_pairs={{32,64},{96,128},{160,192},{224,256},{288,320},{352,384},{416,448}... | collective-permute-start | bytes 430088 | tf_op jit(solution)/shard_map/ppermute | solution.py:434
  49.1 4.0 %collective-permute-start.7 = (bf16[560,128]{1,0:T(8,128)(2,1)S(1)}, bf16[560,128]{1,0:T(8,128)(2,1)S(1)}, u32[]{:S(2)}, u32[]{:S(2)}) collective-permute-start(bf16[560,128]{1,0:T(8,128)(2,1)S(1)} %get-tuple-element.16), channel_id=1, source_target_pairs={{0,32},{64,96},{128,160},{192,224},{256,288},{320,352},{384,416},{... | collective-permute-start | bytes 430088 | tf_op jit(solution)/shard_map/ppermute | solution.py:435
  53.1 1.9 %collective-permute-done.3.vrelay_ref = bf16[512,128]{1,0:T(8,128)(2,1)} collective-permute-done((bf16[512,128]{1,0:T(8,128)(2,1)}, bf16[512,128]{1,0:T(8,128)(2,1)}, u32[]{:S(2)}, u32[]{:S(2)}) %collective-permute-start.3) | collective-permute-done | bytes 131104 | tf_op jit(solution)/shard_map/ppermute | solution.py:430
  55.0 11.8 %own_rows.1 = (bf16[2048,128]{1,0:T(8,128)(2,1)}, bf16[2048,128]{1,0:T(8,128)(2,1)}, bf16[2048,128]{1,0:T(8,128)(2,1)}, f32[1024,128]{1,0:T(8,128)S(1)}, f32[1024,128]{1,0:T(8,128)S(1)}) custom-call(s32[2]{0:T(128)S(1)} %pad_add_fusion.where_ref, s32[1]{0:T(128)S(6)} %copy.16.radius_ref, s32[192]{0:T(256)S(1)} %copy-done.4, bf16[2048,128]{1,0:T(8,128)(2,1)S(1)} %copy-done.3, ...), custom_call_target="tpu_custom_call" | custom-call | flops 3355443200 | bytes 3670016 | tf_op jit(solution)/shard_map/own_rows/pallas_call | solution.py:341
  66.9 3.2 %rim_rows.1 = (bf16[2048,128]{1,0:T(8,128)(2,1)}, bf16[2048,128]{1,0:T(8,128)(2,1)}) custom-call(s32[2]{0:T(128)S(1)} %pad_add_fusion.where_ref, s32[1]{0:T(128)S(6)} %copy.16.radius_ref, s32[192]{0:T(256)S(1)} %copy-done.4, bf16[2048,128]{1,0:T(8,128)(2,1)S(1)} %copy-done.1, ...), custom_call_target="tpu_custom_call", output_to_operand_aliasing={{0}: (12, {}), {1}: (13, {})} | custom-call | flops 402653184 | bytes 1572864 | tf_op jit(solution)/shard_map/rim_rows/pallas_call | solution.py:371
  (15 shorter events, 0.1 us)
Async XLA Ops:
  0.6 1.0 %copy-start = (bf16[64,4096]{1,0:T(8,128)(2,1)S(1)}, bf16[64,4096]{1,0:T(8,128)(2,1)}, u32[]{:S(2)}) copy-start(bf16[64,4096]{1,0:T(8,128)(2,1)} %param.9) | copy-start | bytes 1572868
  2.6 10.6 %copy-start.1 = (bf16[2048,128]{1,0:T(8,128)(2,1)S(1)}, bf16[2048,128]{1,0:T(8,128)(2,1)}, u32[]{:S(2)}) copy-start(bf16[2048,128]{1,0:T(8,128)(2,1)} %k_ref.5) | copy-start | bytes 1572868
  2.6 36.7 %all-to-all-start = ((bf16[64,32,128]{2,0,1:T(8,128)(2,1)}), bf16[64,32,128]{2,0,1:T(8,128)(2,1)S(1)}, u32[]{:S(2)}, u32[]{:S(2)}) async-start(bf16[64,32,128]{2,0,1:T(8,128)(2,1)} %copy_bitcast_fusion), calls=%async_computation | async-start | bytes 1048576 | tf_op jit(solution)/shard_map/all_to_all | solution.py:424
  13.2 1.1 %copy-start.3 = (bf16[2048,128]{1,0:T(8,128)(2,1)S(1)}, bf16[2048,128]{1,0:T(8,128)(2,1)}, u32[]{:S(2)}) copy-start(bf16[2048,128]{1,0:T(8,128)(2,1)} %q_ref.3) | copy-start | bytes 1572868
  13.2 1.2 %copy-start.2 = (bf16[2048,128]{1,0:T(8,128)(2,1)S(1)}, bf16[2048,128]{1,0:T(8,128)(2,1)}, u32[]{:S(2)}) copy-start(bf16[2048,128]{1,0:T(8,128)(2,1)} %v_ref.5) | copy-start | bytes 1572868
  15.3 21.9 %collective-permute-start.4 = (bf16[2048,128]{1,0:T(8,128)(2,1)}, bf16[2048,128]{1,0:T(8,128)(2,1)S(1)}, u32[]{:S(2)}, u32[]{:S(2)}) collective-permute-start(bf16[2048,128]{1,0:T(8,128)(2,1)} %pad_maximum_fusion), channel_id=1, source_target_pairs={{0,32},{64,96},{128,160},{192,224},{256,288},{320,352},{384,416},{... | collective-permute-start | bytes 1572872 | tf_op jit(solution)/shard_map/ppermute | solution.py:427
  18.5 17.3 %collective-permute-start.2 = (bf16[512,128]{1,0:T(8,128)(2,1)S(1)}, bf16[512,128]{1,0:T(8,128)(2,1)}, u32[]{:S(2)}, u32[]{:S(2)}) collective-permute-start(bf16[512,128]{1,0:T(8,128)(2,1)S(1)} %get-tuple-element.24), channel_id=1, source_target_pairs={{224,0},{256,480},{480,256},{512,736},{225,1},{257,481},{481,257},... | collective-permute-start | bytes 393224 | tf_op jit(solution)/shard_map/ppermute | solution.py:426
  22.9 30.2 %collective-permute-start.1 = (bf16[1024,128]{1,0:T(8,128)(2,1)}, bf16[1024,128]{1,0:T(8,128)(2,1)S(1)}, u32[]{:S(2)}, u32[]{:S(2)}) collective-permute-start(bf16[1024,128]{1,0:T(8,128)(2,1)} %pad_maximum_fusion.1), channel_id=1, source_target_pairs={{32,64},{96,128},{160,192},{288,320},{352,384},{416,448},{544,576}... | collective-permute-start | bytes 786440 | tf_op jit(solution)/shard_map/ppermute | solution.py:429
  23.6 25.5 %collective-permute-start = (bf16[512,128]{1,0:T(8,128)(2,1)}, bf16[512,128]{1,0:T(8,128)(2,1)}, u32[]{:S(2)}, u32[]{:S(2)}) collective-permute-start(bf16[512,128]{1,0:T(8,128)(2,1)} %get-tuple-element.22), channel_id=1, source_target_pairs={{32,64},{96,128},{160,192},{224,256},{288,320},{352,384},{416,448}... | collective-permute-start | bytes 393224 | tf_op jit(solution)/shard_map/ppermute | solution.py:428
  35.8 19.2 %collective-permute-start.3 = (bf16[512,128]{1,0:T(8,128)(2,1)}, bf16[512,128]{1,0:T(8,128)(2,1)}, u32[]{:S(2)}, u32[]{:S(2)}) collective-permute-start(bf16[512,128]{1,0:T(8,128)(2,1)} %collective-permute-done.2), channel_id=1, source_target_pairs={{0,256},{480,224},{256,512},{736,480},{1,257},{481,225},{257,513},... | collective-permute-start | bytes 393224 | tf_op jit(solution)/shard_map/ppermute | solution.py:430
  37.9 1.4 %copy-start.4 = (s32[192]{0:T(256)S(1)}, s32[192]{0:T(256)}, u32[]{:S(2)}) copy-start(s32[192]{0:T(256)} %clip_ref.5) | copy-start | bytes 2308
  37.9 29.0 %collective-permute-start.5 = (bf16[512,128]{1,0:T(8,128)(2,1)}, bf16[512,128]{1,0:T(8,128)(2,1)S(1)}, u32[]{:S(2)}, u32[]{:S(2)}) collective-permute-start(bf16[512,128]{1,0:T(8,128)(2,1)} %slice.4), channel_id=1, source_target_pairs={{192,256},{288,224},{448,512},{544,480},{193,257},{289,225},{449,5... | collective-permute-start | bytes 393224 | tf_op jit(solution)/shard_map/ppermute | solution.py:431
  41.2 25.7 %collective-permute-start.6 = (bf16[560,128]{1,0:T(8,128)(2,1)S(1)}, bf16[560,128]{1,0:T(8,128)(2,1)S(1)}, u32[]{:S(2)}, u32[]{:S(2)}) collective-permute-start(bf16[560,128]{1,0:T(8,128)(2,1)S(1)} %get-tuple-element.15), channel_id=1, source_target_pairs={{32,64},{96,128},{160,192},{224,256},{288,320},{352,384},{416,448}... | collective-permute-start | bytes 430088 | tf_op jit(solution)/shard_map/ppermute | solution.py:434
  49.1 17.8 %collective-permute-start.7 = (bf16[560,128]{1,0:T(8,128)(2,1)S(1)}, bf16[560,128]{1,0:T(8,128)(2,1)S(1)}, u32[]{:S(2)}, u32[]{:S(2)}) collective-permute-start(bf16[560,128]{1,0:T(8,128)(2,1)S(1)} %get-tuple-element.16), channel_id=1, source_target_pairs={{0,32},{64,96},{128,160},{192,224},{256,288},{320,352},{384,416},{... | collective-permute-start | bytes 430088 | tf_op jit(solution)/shard_map/ppermute | solution.py:435
